TPU v7x, 256 devices: a whole 4x4x8 slice. The times are simulated.
256 devices in a mesh: star: 8 (over x, core), row: 32 (over z, y).
Axes of the slice: x: 4, y: 4, z: 8, core: 2. Of those that a mesh axis runs over, the one named last changes fastest.
Arguments:
- feature_maps: bfloat16 [64, 1024, 1024], P(None, 'row'), may hold values from -6 to 6
- coef_table: bfloat16 [64, 64], replicated, may hold values from -0.119628906 to 0.119628906
- star_counts: int32 [8], replicated, may hold values from 1 to 12, 32 in all
- star_cells: int32 [8, 12], replicated, may hold values from 0 to 63
- star_bands: int32 [8, 12], replicated, may hold values from 0 to 7
- psf_cotangent: bfloat16 [96, 1024, 1024], P('star', 'row'), may hold values from -6 to 6
Outputs:
- map_grad: float32 [64, 1024, 1024], P('star', 'row')
- coef_grad: float32 [64, 64], replicated
Inputs may be any that keep to these rules, and one draw needn't show every extreme that they name: The live stars of group g fill its slots 0 to star_counts[g] - 1; the counts sum to 32, and some group has exactly 12.
All inputs are finite; a program needn't handle non-finite values.
Results may differ from a plain program's by a relative error of at most 0.008.
Values may be sent and summed in bfloat16 or wider, within the bound.
No kernel may reach another device: no remote copies, remote signals or barrier semaphores. Data moves between devices by JAX's collectives and lax.ppermute only.
A program may use at most 128 MiB of HBM per device.

v0:
```python
import jax
import jax.numpy as jnp
from jax import lax
from jax.sharding import PartitionSpec as P

BANDS = 8


def fourier_tables(pupil_size):
    index_row = jnp.arange(pupil_size, dtype=jnp.int32)
    products = index_row[:, None] * index_row[None, :] % pupil_size
    angles = 2.0 * jnp.pi / pupil_size * products.astype(jnp.float32)
    return (jnp.cos(angles).astype(jnp.bfloat16), (-jnp.sin(angles)).astype(jnp.bfloat16))


def aperture_rows(first_row, row_count, pupil_size):
    centre = 0.5 * (pupil_size - 1)
    row_pos = (first_row + jnp.arange(row_count, dtype=jnp.int32)).astype(jnp.float32) - centre
    col_pos = jnp.arange(pupil_size, dtype=jnp.int32).astype(jnp.float32) - centre
    radius = row_pos[:, None] * row_pos[:, None] + col_pos[None, :] * col_pos[None, :]
    return jnp.where(radius <= 0.25 * pupil_size * pupil_size, 1.0, 0.0).astype(jnp.float32)


def wave_numbers(band_ids):
    wavelength = 0.55 + 0.35 * band_ids.astype(jnp.float32) / (BANDS - 1)
    return 2.0 * jnp.pi / wavelength


def table_pick(values, indices):
    positions = jnp.arange(values.shape[0], dtype=jnp.int32)
    chosen = jnp.where(positions[None, :] == indices[:, None], values[None, :], 0)
    return jnp.sum(chosen, axis=1)


def per_device(feature_maps, coef_table, star_counts, star_cells, star_bands, psf_cotangent):
    groups = lax.axis_size("star")
    my_group = lax.axis_index("star")
    slot_count = psf_cotangent.shape[0]
    map_count, row_count, pupil_size = feature_maps.shape
    flat_cells = star_cells.reshape(-1)
    flat_bands = star_bands.reshape(-1)
    cell_count = coef_table.shape[0]
    within = jnp.arange(slot_count, dtype=jnp.int32)
    owner_group = jnp.zeros_like(within) + my_group
    live_mask = within < table_pick(star_counts, owner_group)
    owner_group, within, live_mask = (owner_group, within, live_mask)
    slot_index = owner_group * slot_count + within
    cell_ids = table_pick(flat_cells, slot_index)
    band_ids = table_pick(flat_bands, slot_index)
    cell_hot = cell_ids[:, None] == jnp.arange(cell_count, dtype=jnp.int32)[None, :]
    coef_rows = jnp.dot(
        cell_hot.astype(jnp.bfloat16), coef_table, preferred_element_type=jnp.float32
    ).astype(jnp.bfloat16)
    flat_maps = feature_maps.reshape(map_count, row_count * pupil_size)
    path_error = jnp.dot(coef_rows, flat_maps, preferred_element_type=jnp.float32).reshape(
        -1, row_count, pupil_size
    )
    wave_number = wave_numbers(band_ids)
    phase_angle = wave_number[:, None, None] * path_error
    aperture = aperture_rows(lax.axis_index("row") * row_count, row_count, pupil_size)
    cos_phase = jnp.cos(phase_angle)
    sin_phase = jnp.sin(phase_angle)
    pupil_field = jnp.stack([aperture * cos_phase, aperture * sin_phase], 1).astype(jnp.bfloat16)
    cos_table, sin_table = fourier_tables(pupil_size)
    inverse = 1.0 / pupil_size
    along_cos = jnp.einsum(
        "sarc,cv->sarv", pupil_field, cos_table, preferred_element_type=jnp.float32
    )
    along_sin = jnp.einsum(
        "sarc,cv->sarv", pupil_field, sin_table, preferred_element_type=jnp.float32
    )
    column_field = jnp.stack(
        [along_cos[:, 0] - along_sin[:, 1], along_sin[:, 0] + along_cos[:, 1]], 1
    ).astype(jnp.bfloat16)
    pieces = lax.all_to_all(column_field, "row", split_axis=3, concat_axis=2, tiled=True)
    row_cos = jnp.einsum("sarv,ru->savu", pieces, cos_table, preferred_element_type=jnp.float32)
    row_sin = jnp.einsum("sarv,ru->savu", pieces, sin_table, preferred_element_type=jnp.float32)
    real_part = (row_cos[:, 0] - row_sin[:, 1]) * inverse
    imag_part = (row_sin[:, 0] + row_cos[:, 1]) * inverse
    focal_field = jnp.stack([real_part, imag_part], 1)
    weight = jnp.where(live_mask, 2.0, 0.0).astype(jnp.float32)[:, None, None, None]
    focal_grad = (weight * psf_cotangent.astype(jnp.float32)[:, None] * focal_field).astype(
        jnp.bfloat16
    )
    back_cos = jnp.einsum(
        "savu,ur->savr", focal_grad, cos_table, preferred_element_type=jnp.float32
    )
    back_sin = jnp.einsum(
        "savu,ur->savr", focal_grad, sin_table, preferred_element_type=jnp.float32
    )
    spectrum_grad = jnp.stack(
        [(back_cos[:, 0] + back_sin[:, 1]) * inverse, (back_cos[:, 1] - back_sin[:, 0]) * inverse],
        1,
    ).astype(jnp.bfloat16)
    pieces = lax.all_to_all(spectrum_grad, "row", split_axis=3, concat_axis=2, tiled=True)
    col_cos = jnp.einsum("savr,vc->sarc", pieces, cos_table, preferred_element_type=jnp.float32)
    col_sin = jnp.einsum("savr,vc->sarc", pieces, sin_table, preferred_element_type=jnp.float32)
    pupil_grad = jnp.stack([col_cos[:, 0] + col_sin[:, 1], col_cos[:, 1] - col_sin[:, 0]], 1)
    phase_grad = aperture * (cos_phase * pupil_grad[:, 1] - sin_phase * pupil_grad[:, 0])
    path_grad = (
        (wave_number[:, None, None] * phase_grad)
        .astype(jnp.bfloat16)
        .reshape(-1, row_count * pupil_size)
    )
    map_scores = lax.dot_general(
        path_grad, flat_maps, (((1,), (1,)), ((), ())), preferred_element_type=jnp.float32
    )
    coef_part = lax.dot_general(
        cell_hot.astype(jnp.float32),
        map_scores * (1.0 / (8 * pupil_size)),
        (((0,), (0,)), ((), ())),
        precision=lax.Precision.HIGHEST,
    )
    coef_grad = lax.psum(coef_part, ("star", "row"))
    share = map_count // groups
    map_grad = lax.psum_scatter(
        lax.dot_general(
            coef_rows, path_grad, (((0,), (0,)), ((), ())), preferred_element_type=jnp.float32
        ),
        "star",
        scatter_dimension=0,
        tiled=True,
    )
    return (map_grad.reshape(share, row_count, pupil_size), coef_grad)


def solution(mesh):
    placed = (P(None, "row", None), P(), P(), P(), P(), P("star", "row", None))
    return jax.shard_map(
        per_device,
        mesh=mesh,
        in_specs=placed,
        out_specs=(P("star", "row", None), P()),
        check_vma=False,
    )
```

profile of v0, /device:TPU:1, one launch (start us, length us, event | category | flops | bytes accessed | tf_op | source)
XLA Modules:
  0.0 501.8 jit_solution(5607141360308045111)
XLA Ops:
  9.2 6.7 %fusion.3 = f32[12,32,1024]{2,0,1:T(8,128)S(1)} fusion(bf16[12,64]{1,0:T(8,128)(2,1)S(1)} %convolution_convert_fusion, bf16[8,8,32,1024]{3,2,1,0:T(8,128)(2,1)} %bitcast.95), kind=kOutput, calls=%fused_computation.8 | convolution fusion | flops 50331648 | bytes 5768704 | tf_op jit(solution)/shard_map/dot_general | solution.py:55
  16.0 8.4 %fusion.54 = (bf16[12,1,32,1024]{3,0,2,1:T(8,128)(2,1)S(1)}, bf16[12,1,32,1024]{3,0,2,1:T(8,128)(2,1)S(1)}) fusion(f32[12,32,1024]{2,0,1:T(8,128)S(1)} %fusion.3, f32[32,1024]{1,0:T(8,128)S(1)} %fusion.56, f32[12]{0:T(128)S(1)} %add_divide_fusion), kind=kLoop, calls=%fused_computation.67 | loop fusion | flops 1966080 | bytes 3276848 | tf_op jit(solution)/shard_map/stack | solution.py:63
  24.7 17.9 %fusion.28 = f32[12,2,32,1024]{3,2,1,0:T(8,128)S(1)} fusion(bf16[12,2,32,1024]{3,0,2,1:T(8,128)(2,1)S(1)} %pad_maximum_fusion), kind=kOutput, calls=%fused_computation.36 | convolution fusion | flops 1627389952 | bytes 4718592 | tf_op jit(solution)/shard_map/sarc,cv->sarv/dot_general | solution.py:69
  42.5 17.3 %fusion.36 = f32[12,2,32,1024]{3,2,1,0:T(8,128)S(1)} fusion(bf16[12,2,32,1024]{3,0,2,1:T(8,128)(2,1)S(1)} %pad_maximum_fusion), kind=kOutput, calls=%fused_computation.40 | convolution fusion | flops 1626341376 | bytes 4718592 | tf_op jit(solution)/shard_map/sarc,cv->sarv/dot_general | solution.py:66
  59.9 1.2 fusion.45
  61.1 1.3 pad_maximum_fusion.1
  62.4 15.1 %copy.45 = bf16[12,2,32,1024]{2,1,0,3:T(2,128)(2,1)} copy(bf16[12,2,32,1024]{3,2,1,0:T(8,128)(2,1)} %pad_maximum_fusion.1) | data formatting | bytes 3145728 | tf_op jit(solution)/shard_map/stack | solution.py:72
  77.5 13.8 %reshape.93 = bf16[32,2,12288]{2,1,0:T(2,128)(2,1)} reshape(bf16[1024,12,2,32]{3,2,1,0:T(2,128)(2,1)} %bitcast.93) | data formatting | bytes 3145728
  91.3 12.3 %all-to-all-start = ((bf16[32,2,12288]{2,1,0:T(2,128)(2,1)}), bf16[32,2,12288]{2,1,0:T(2,128)(2,1)}, u32[]{:S(2)}, u32[]{:S(2)}) async-start(bf16[32,2,12288]{2,1,0:T(2,128)(2,1)} %reshape.93), calls=%async_computation | async-start | bytes 3145728 | tf_op jit(solution)/shard_map/all_to_all | solution.py:75
  103.8 1.4 convert_multiply_fusion
  105.2 36.3 %all-to-all-done = bf16[32,2,12288]{2,1,0:T(2,128)(2,1)} async-done(((bf16[32,2,12288]{2,1,0:T(2,128)(2,1)}), bf16[32,2,12288]{2,1,0:T(2,128)(2,1)}, u32[]{:S(2)}, u32[]{:S(2)}) %all-to-all-start) | async-done | bytes 1572896 | tf_op jit(solution)/shard_map/all_to_all | solution.py:75
  141.5 14.3 %reshape.94 = bf16[1024,12,2,32]{3,2,1,0:T(2,128)(2,1)} reshape(bf16[32,2,12288]{2,1,0:T(2,128)(2,1)} %all-to-all-done) | data formatting | bytes 3145728
  155.7 9.5 %copy.107 = bf16[12,2,32,32,32]{2,3,4,1,0:T(8,128)(2,1)} copy(bf16[12,2,32,32,32]{2,1,0,4,3:T(2,128)(2,1)} %bitcast.89) | data formatting | bytes 3145728 | tf_op jit(solution)/shard_map/all_to_all | solution.py:75
  165.2 9.8 %all_to_all.29 = bf16[12,2,1024,32]{2,3,1,0:T(8,128)(2,1)} reshape(bf16[12,2,32,32,32]{3,2,4,1,0:T(8,128)(2,1)} %bitcast.90) | data formatting | bytes 3145728 | tf_op jit(solution)/shard_map/all_to_all | solution.py:75
  175.0 18.3 %fusion.26 = f32[12,2,32,1024]{3,2,1,0:T(8,128)S(1)} fusion(bf16[12,2,1024,32]{2,3,1,0:T(8,128)(2,1)} %all_to_all.29), kind=kOutput, calls=%fused_computation.35 | convolution fusion | flops 1627389952 | bytes 4718592 | tf_op jit(solution)/shard_map/sarv,ru->savu/dot_general | solution.py:77
  193.3 17.4 %fusion.34 = f32[12,2,32,1024]{3,2,1,0:T(8,128)S(1)} fusion(bf16[12,2,1024,32]{2,3,1,0:T(8,128)(2,1)S(1)} %copy-done.3), kind=kOutput, calls=%fused_computation.39 | convolution fusion | flops 1626341376 | bytes 4718592 | tf_op jit(solution)/shard_map/sarv,ru->savu/dot_general | solution.py:76
  212.1 16.4 %fusion.32 = f32[12,2,32,1024]{3,2,1,0:T(8,128)S(1)} fusion(f32[12,1,32,1024]{3,2,1,0:T(8,128)S(1)} %get-tuple-element.15, f32[12,1,32,1024]{3,2,1,0:T(8,128)S(1)} %get-tuple-element.14, f32[12,32,1024]{2,1,0:T(8,128)S(1)} %copy-done.2), kind=kOutput, calls=%fused_computation.38 | convolution fusion | flops 1628700672 | bytes 7864320 | tf_op jit(solution)/shard_map/savu,ur->savr/dot_general | solution.py:85
  228.5 16.7 %fusion.24 = f32[12,2,32,1024]{3,2,1,0:T(8,128)S(1)} fusion(f32[12,1,32,1024]{3,2,1,0:T(8,128)S(1)} %get-tuple-element.15, f32[12,1,32,1024]{3,2,1,0:T(8,128)S(1)} %get-tuple-element.14, f32[12,32,1024]{2,1,0:T(8,128)S(1)} %copy-done.2), kind=kOutput, calls=%fused_computation.34 | convolution fusion | flops 1629749248 | bytes 7864320 | tf_op jit(solution)/shard_map/savu,ur->savr/dot_general | solution.py:88
  246.0 1.3 pad_maximum_fusion.2
  247.2 15.1 %copy.47 = bf16[12,2,32,1024]{2,1,0,3:T(2,128)(2,1)} copy(bf16[12,2,32,1024]{3,2,1,0:T(8,128)(2,1)} %pad_maximum_fusion.2) | data formatting | bytes 3145728 | tf_op jit(solution)/shard_map/stack | solution.py:91
  262.3 14.2 %reshape.95 = bf16[32,2,12288]{2,1,0:T(2,128)(2,1)} reshape(bf16[1024,12,2,32]{3,2,1,0:T(2,128)(2,1)} %bitcast.94) | data formatting | bytes 3145728
  276.5 42.9 %all_to_all.36 = bf16[32,2,12288]{2,1,0:T(2,128)(2,1)} all-to-all(bf16[32,2,12288]{2,1,0:T(2,128)(2,1)} %reshape.95), channel_id=1, replica_groups=mesh['star'=8,'row'=32] {'row'}, dimensions={0} | all-to-all | bytes 3145728 | tf_op jit(solution)/shard_map/all_to_all | solution.py:95
  319.5 14.3 %reshape.96 = bf16[1024,12,2,32]{3,2,1,0:T(2,128)(2,1)} reshape(bf16[32,2,12288]{2,1,0:T(2,128)(2,1)} %all_to_all.36) | data formatting | bytes 3145728
  333.7 9.5 %copy.106 = bf16[12,2,32,32,32]{2,3,4,1,0:T(8,128)(2,1)} copy(bf16[12,2,32,32,32]{2,1,0,4,3:T(2,128)(2,1)} %bitcast.91) | data formatting | bytes 3145728 | tf_op jit(solution)/shard_map/all_to_all | solution.py:95
  343.2 9.8 %all_to_all.33 = bf16[12,2,1024,32]{2,3,1,0:T(8,128)(2,1)} reshape(bf16[12,2,32,32,32]{3,2,4,1,0:T(8,128)(2,1)} %bitcast.92) | data formatting | bytes 3145728 | tf_op jit(solution)/shard_map/all_to_all | solution.py:95
  353.0 18.3 %fusion.22 = f32[12,2,32,1024]{3,2,1,0:T(8,128)S(1)} fusion(bf16[12,2,1024,32]{2,3,1,0:T(8,128)(2,1)} %all_to_all.33), kind=kOutput, calls=%fused_computation.33 | convolution fusion | flops 1627389952 | bytes 4718592 | tf_op jit(solution)/shard_map/savr,vc->sarc/dot_general | solution.py:97
  371.3 17.0 %fusion.30 = f32[12,2,32,1024]{3,2,1,0:T(8,128)S(1)} fusion(bf16[12,2,1024,32]{2,3,1,0:T(8,128)(2,1)S(1)} %copy-done.4), kind=kOutput, calls=%fused_computation.37 | convolution fusion | flops 1626341376 | bytes 4718592 | tf_op jit(solution)/shard_map/savr,vc->sarc/dot_general | solution.py:96
  389.4 11.4 %fusion.19 = bf16[12,32,1024]{2,0,1:T(8,128)(2,1)S(1)} fusion(f32[12,1,32,1024]{3,2,1,0:T(8,128)S(1)} %get-tuple-element.24, f32[12,1,32,1024]{3,2,1,0:T(8,128)S(1)} %get-tuple-element.19, f32[12,1,32,1024]{3,2,1,0:T(8,128)S(1)} %get-tuple-element.25, f32[12,1,32,1024]{3,2,1,0:T(8,128)S(1)} %get-tuple-element.18, f32[12,32,1024]{2,0,1:T(8,128)S(1)} %fusion.3, ...), kind=kLoop, calls=%fused_computation.29 | loop fusion | flops 3538944 | bytes 8781872 | tf_op jit(solution)/shard_map/convert_element_type | solution.py:102
  402.0 4.5 fusion.97
  406.5 6.8 %fusion.51 = f32[12,64]{1,0:T(8,128)S(1)} fusion(bf16[12,32,1024]{2,0,1:T(8,128)(2,1)S(1)} %fusion.19, bf16[64,32,1024]{2,1,0:T(8,128)(2,1)} %param.6), kind=kOutput, calls=%fused_computation.65 | convolution fusion | flops 50332416 | bytes 4983808 | tf_op jit(solution)/shard_map/dot_general | solution.py:105
  413.6 78.1 %psum.7 = f32[64,64]{1,0:T(8,128)} all-reduce(f32[64,64]{1,0:T(8,128)S(1)} %fusion.57), channel_id=1, replica_groups=mesh['star'=8,'row'=32] {'star','row'}, use_global_device_ids=true, to_apply=%region_4.5 | all-reduce | flops 4096 | bytes 32768 | tf_op jit(solution)/shard_map/psum | solution.py:114
  491.7 2.8 copy.55
  (36 shorter events, 7.2 us)
Async XLA Ops:
  7.2 1.8 copy-start
  91.3 12.3 %copy-start.6 = (s32[8]{0:T(128)S(1)}, s32[8]{0:T(128)}, u32[]{:S(2)}) copy-start(s32[8]{0:T(128)} %param.8) | copy-start | bytes 100
  91.3 12.4 %copy-start.5 = (bf16[12,32,1024]{2,1,0:T(8,128)(2,1)S(1)}, bf16[12,32,1024]{2,1,0:T(8,128)(2,1)}, u32[]{:S(2)}) copy-start(bf16[12,32,1024]{2,1,0:T(8,128)(2,1)} %param.11) | copy-start | bytes 2359300
  91.3 50.2 %all-to-all-start = ((bf16[32,2,12288]{2,1,0:T(2,128)(2,1)}), bf16[32,2,12288]{2,1,0:T(2,128)(2,1)}, u32[]{:S(2)}, u32[]{:S(2)}) async-start(bf16[32,2,12288]{2,1,0:T(2,128)(2,1)} %reshape.93), calls=%async_computation | async-start | bytes 3145728 | tf_op jit(solution)/shard_map/all_to_all | solution.py:75
  103.6 388.1 %reduce-scatter.2.cloned.1.call-start = ((), (), s32[]{:S(2)}) async-start(), calls=%async_computation.3 | async-start | bytes 9437184 | tf_op jit(solution)/shard_map/reduce_scatter | solution.py:116
  175.0 18.3 %copy-start.3 = (bf16[12,2,1024,32]{2,3,1,0:T(8,128)(2,1)S(1)}, bf16[12,2,1024,32]{2,3,1,0:T(8,128)(2,1)}, u32[]{:S(2)}) copy-start(bf16[12,2,1024,32]{2,3,1,0:T(8,128)(2,1)} %all_to_all.29) | copy-start | bytes 4718596
  210.7 1.4 copy-start.2
  353.0 18.3 %copy-start.4 = (bf16[12,2,1024,32]{2,3,1,0:T(8,128)(2,1)S(1)}, bf16[12,2,1024,32]{2,3,1,0:T(8,128)(2,1)}, u32[]{:S(2)}) copy-start(bf16[12,2,1024,32]{2,3,1,0:T(8,128)(2,1)} %all_to_all.33) | copy-start | bytes 4718596
  406.5 88.0 %copy-start.1 = (bf16[64,64]{1,0:T(8,128)(2,1)S(1)}, bf16[64,64]{1,0:T(8,128)(2,1)}, u32[]{:S(2)}) copy-start(bf16[64,64]{1,0:T(8,128)(2,1)} %param.7) | copy-start | bytes 24580
Sparse Core Ops, SparseCore 0:
  406.6 54.6 reduce-scatter.1
where the time goes:
time: 509 us; the launch traced here: 502 us
  matrix products  158 us (31%)
  local copies, waits for them, and re-layouts  132 us (26%)
  blocking collectives  121 us (24%)
  waiting for transfers between devices  36.3 us (7%)
  other arithmetic  27.5 us (5%)
  between operations  14.7 us (3%)
  starting transfers between devices  12.3 us (2%)
    psum x1, blocking collectives, per_device(): coef_grad = lax.psum(coef_part, ('star', 'row'))  78.1 us
    unnamed x21, local copies, waits for them, and re-layouts  60.5 us
    all_to_all x1, blocking collectives, per_device(): lax.all_to_all(spectrum_grad, 'row', split_axis=3, concat_axis=2, tiled=T...  42.9 us
    all_to_all x1, waiting for transfers between devices, per_device(): lax.all_to_all(column_field, 'row', split_axis=3, concat_axis=2, tiled=True)  36.3 us
    all_to_all x2, local copies, waits for them, and re-layouts, per_device(): lax.all_to_all(column_field, 'row', split_axis=3, concat_axis=2, tiled=True)  19.3 us
    all_to_all x2, local copies, waits for them, and re-layouts, per_device(): lax.all_to_all(spectrum_grad, 'row', split_axis=3, concat_axis=2, tiled=T...  19.3 us
    dot_general x1, matrix products, per_device(): jnp.einsum('savr,vc->sarc', pieces, sin_table, preferred_element_type=jnp...  18.3 us
    dot_general x1, matrix products, per_device(): jnp.einsum('sarv,ru->savu', pieces, sin_table, preferred_element_type=jnp...  18.3 us
  transfers between devices with their start and end apart: 2, of which 1 were waited for; matrix products, arithmetic and copies ran while one was open for 2% of the time, Pallas kernels for 0%

commit v1 on v0

--- a/solution.py
+++ b/solution.py
@@ -92,7 +92,12 @@
         [(back_cos[:, 0] + back_sin[:, 1]) * inverse, (back_cos[:, 1] - back_sin[:, 0]) * inverse],
         1,
     ).astype(jnp.bfloat16)
-    pieces = lax.all_to_all(spectrum_grad, "row", split_axis=3, concat_axis=2, tiled=True)
+    pieces = jnp.concatenate(
+        lax.all_to_all(
+            jnp.stack(jnp.split(spectrum_grad, lax.axis_size("row"), axis=3)), "row", 0, 0
+        ),
+        axis=2,
+    )
     col_cos = jnp.einsum("savr,vc->sarc", pieces, cos_table, preferred_element_type=jnp.float32)
     col_sin = jnp.einsum("savr,vc->sarc", pieces, sin_table, preferred_element_type=jnp.float32)
     pupil_grad = jnp.stack([col_cos[:, 0] + col_sin[:, 1], col_cos[:, 1] - col_sin[:, 0]], 1)

time: 509 us -> 486 us (0.955)
  local copies, waits for them, and re-layouts: 132 us -> 90.2 us
  other arithmetic: 27.5 us -> 50 us
    unnamed x0 -> x31, other arithmetic: none -> 24.5 us
    unnamed x21 -> x17, local copies, waits for them, and re-layouts: 60.5 us -> 37.1 us
    reshape x0 -> x2, local copies, waits for them, and re-layouts: none -> 20.5 us  [per_device(): jnp.concatenate(lax.all_to_all(jnp.stack(jnp.split(spectrum_grad, lax.axi...]
    all_to_all x2 -> x0, local copies, waits for them, and re-layouts: 19.3 us -> none  [per_device(): lax.all_to_all(spectrum_grad, 'row', split_axis=3, concat_axis=2, tiled=T...]
    another operation x1 -> x0, local copies, waits for them, and re-layouts: 15.1 us -> none  [per_device(): jnp.stack([(back_cos[:, 0] + back_sin[:, 1]) * inverse, (back_cos[:, 1] -...]
where the time goes in v1:
time: 486 us; the launch traced here: 480 us
  matrix products  156 us (32%)
  blocking collectives  121 us (25%)
  local copies, waits for them, and re-layouts  90.2 us (19%)
  other arithmetic  50 us (10%)
  waiting for transfers between devices  36.4 us (7%)
  between operations  14.5 us (3%)
  starting transfers between devices  12.1 us (2%)
    psum x1, blocking collectives, per_device(): coef_grad = lax.psum(coef_part, ('star', 'row'))  78.2 us
    all_to_all x1, blocking collectives, per_device(): lax.all_to_all(jnp.stack(jnp.split(spectrum_grad, lax.axis_size('row'), a...  42.6 us
    unnamed x17, local copies, waits for them, and re-layouts  37.1 us
    all_to_all x1, waiting for transfers between devices, per_device(): lax.all_to_all(column_field, 'row', split_axis=3, concat_axis=2, tiled=True)  36.3 us
    unnamed x31, other arithmetic  24.5 us
    reshape x2, local copies, waits for them, and re-layouts, per_device(): jnp.concatenate(lax.all_to_all(jnp.stack(jnp.split(spectrum_grad, lax.axi...  20.5 us
    all_to_all x2, local copies, waits for them, and re-layouts, per_device(): lax.all_to_all(column_field, 'row', split_axis=3, concat_axis=2, tiled=True)  18.2 us
    dot_general x1, matrix products, per_device(): jnp.einsum('sarc,cv->sarv', pupil_field, sin_table, preferred_element_typ...  17.6 us
  transfers between devices with their start and end apart: 2, of which 1 were waited for; matrix products, arithmetic and copies ran while one was open for 2% of the time, Pallas kernels for 0%

profile of v1, /device:TPU:1, one launch (start us, length us, event | category | flops | bytes accessed | tf_op | source)
XLA Modules:
  0.0 480.1 jit_solution(8144197037946635837)
XLA Ops:
  9.2 6.7 %fusion.3 = f32[12,32,1024]{2,0,1:T(8,128)S(1)} fusion(bf16[12,64]{1,0:T(8,128)(2,1)S(1)} %convolution_convert_fusion, bf16[8,8,32,1024]{3,2,1,0:T(8,128)(2,1)} %bitcast.154), kind=kOutput, calls=%fused_computation.69 | convolution fusion | flops 50331648 | bytes 5768704 | tf_op jit(solution)/shard_map/dot_general | solution.py:55
  16.0 1.3 copy-done.2
  17.3 8.7 %fusion.54 = (bf16[12,1,32,1024]{3,0,2,1:T(8,128)(2,1)S(1)}, bf16[12,1,32,1024]{3,0,2,1:T(8,128)(2,1)S(1)}) fusion(f32[12,32,1024]{2,0,1:T(8,128)S(1)} %fusion.3, f32[32,1024]{1,0:T(8,128)S(1)} %fusion.89, f32[12]{0:T(128)S(1)} %add_divide_fusion), kind=kLoop, calls=%fused_computation.127 | loop fusion | flops 1966080 | bytes 3276848 | tf_op jit(solution)/shard_map/stack | solution.py:63
  26.3 17.6 %fusion.28 = f32[12,2,32,1024]{3,2,1,0:T(8,128)S(1)} fusion(bf16[12,2,32,1024]{3,0,2,1:T(8,128)(2,1)S(1)} %pad_maximum_fusion), kind=kOutput, calls=%fused_computation.97 | convolution fusion | flops 1627389952 | bytes 4718592 | tf_op jit(solution)/shard_map/sarc,cv->sarv/dot_general | solution.py:69
  43.9 17.6 %fusion.36 = f32[12,2,32,1024]{3,2,1,0:T(8,128)S(1)} fusion(bf16[12,2,32,1024]{3,0,2,1:T(8,128)(2,1)S(1)} %pad_maximum_fusion), kind=kOutput, calls=%fused_computation.101 | convolution fusion | flops 1626341376 | bytes 4718592 | tf_op jit(solution)/shard_map/sarc,cv->sarv/dot_general | solution.py:66
  61.5 1.0 fusion.45
  62.7 11.3 %copy.43 = bf16[12,2,32,1024]{2,1,0,3:T(2,128)(2,1)} copy(bf16[12,2,32,1024]{3,2,1,0:T(8,128)(2,1)S(1)} %pad_maximum_fusion.1) | data formatting | bytes 3145728 | tf_op jit(solution)/shard_map/stack | solution.py:72
  73.9 13.8 %reshape.101 = bf16[32,2,12288]{2,1,0:T(2,128)(2,1)} reshape(bf16[1024,12,2,32]{3,2,1,0:T(2,128)(2,1)} %bitcast.153) | data formatting | bytes 3145728
  87.8 12.0 %all-to-all-start = ((bf16[32,2,12288]{2,1,0:T(2,128)(2,1)}), bf16[32,2,12288]{2,1,0:T(2,128)(2,1)S(1)}, u32[]{:S(2)}, u32[]{:S(2)}) async-start(bf16[32,2,12288]{2,1,0:T(2,128)(2,1)} %reshape.101), calls=%async_computation | async-start | bytes 3145728 | tf_op jit(solution)/shard_map/all_to_all | solution.py:75
  100.0 1.4 convert_multiply_fusion
  101.3 36.3 %all-to-all-done = bf16[32,2,12288]{2,1,0:T(2,128)(2,1)S(1)} async-done(((bf16[32,2,12288]{2,1,0:T(2,128)(2,1)}), bf16[32,2,12288]{2,1,0:T(2,128)(2,1)S(1)}, u32[]{:S(2)}, u32[]{:S(2)}) %all-to-all-start) | async-done | bytes 1572896 | tf_op jit(solution)/shard_map/all_to_all | solution.py:75
  137.7 4.6 reshape.102
  142.3 9.5 %copy.102 = bf16[12,2,32,32,32]{2,3,4,1,0:T(8,128)(2,1)} copy(bf16[12,2,32,32,32]{2,1,0,4,3:T(2,128)(2,1)} %bitcast.150) | data formatting | bytes 3145728 | tf_op jit(solution)/shard_map/all_to_all | solution.py:75
  151.8 8.8 %all_to_all.19 = bf16[12,2,1024,32]{2,3,1,0:T(8,128)(2,1)S(1)} reshape(bf16[12,2,32,32,32]{3,2,4,1,0:T(8,128)(2,1)} %bitcast.151) | data formatting | bytes 3145728 | tf_op jit(solution)/shard_map/all_to_all | solution.py:75
  160.5 17.3 %fusion.26 = f32[12,2,32,1024]{3,2,1,0:T(8,128)S(1)} fusion(bf16[12,2,1024,32]{2,3,1,0:T(8,128)(2,1)S(1)} %all_to_all.19), kind=kOutput, calls=%fused_computation.96 | convolution fusion | flops 1627389952 | bytes 4718592 | tf_op jit(solution)/shard_map/sarv,ru->savu/dot_general | solution.py:77
  177.8 17.4 %fusion.34 = f32[12,2,32,1024]{3,2,1,0:T(8,128)S(1)} fusion(bf16[12,2,1024,32]{2,3,1,0:T(8,128)(2,1)S(1)} %all_to_all.19), kind=kOutput, calls=%fused_computation.100 | convolution fusion | flops 1626341376 | bytes 4718592 | tf_op jit(solution)/shard_map/sarv,ru->savu/dot_general | solution.py:76
  195.2 1.0 fusion.43
  196.3 16.6 %fusion.24 = f32[12,2,32,1024]{3,2,1,0:T(8,128)S(1)} fusion(f32[12,1,32,1024]{3,2,1,0:T(8,128)S(1)} %get-tuple-element.15, f32[12,1,32,1024]{3,2,1,0:T(8,128)S(1)} %get-tuple-element.14, f32[12,32,1024]{2,1,0:T(8,128)S(1)} %convert_multiply_fusion), kind=kOutput, calls=%fused_computation.95 | convolution fusion | flops 1629749248 | bytes 7864320 | tf_op jit(solution)/shard_map/savu,ur->savr/dot_general | solution.py:88
  212.9 16.6 %fusion.32 = f32[12,2,32,1024]{3,2,1,0:T(8,128)S(1)} fusion(f32[12,1,32,1024]{3,2,1,0:T(8,128)S(1)} %get-tuple-element.15, f32[12,1,32,1024]{3,2,1,0:T(8,128)S(1)} %get-tuple-element.14, f32[12,32,1024]{2,1,0:T(8,128)S(1)} %convert_multiply_fusion), kind=kOutput, calls=%fused_computation.99 | convolution fusion | flops 1628700672 | bytes 7864320 | tf_op jit(solution)/shard_map/savu,ur->savr/dot_general | solution.py:85
  255.6 8.8 %reshape.103 = bf16[32,2,12288]{2,1,0:T(2,128)(2,1)S(1)} reshape(bf16[32,12,2,32,32]{4,3,2,1,0:T(8,128)(2,1)} %fusion.88) | data formatting | bytes 3145728
  264.4 42.6 %all_to_all.23 = bf16[32,2,12288]{2,1,0:T(2,128)(2,1)S(1)} all-to-all(bf16[32,2,12288]{2,1,0:T(2,128)(2,1)S(1)} %reshape.103), channel_id=1, replica_groups=mesh['star'=8,'row'=32] {'row'}, dimensions={0} | all-to-all | bytes 3145728 | tf_op jit(solution)/shard_map/all_to_all | solution.py:96
  307.0 4.6 reshape.104
  311.6 11.7 %copy.45 = bf16[12,2,32,32,32]{3,2,4,1,0:T(8,128)(2,1)} copy(bf16[12,2,32,32,32]{4,3,1,0,2:T(8,128)(2,1)} %bitcast.152) | data formatting | bytes 3145728 | tf_op jit(solution)/shard_map/reshape | solution.py:95
  323.3 8.8 %reshape.94 = bf16[12,2,1024,32]{2,3,1,0:T(8,128)(2,1)S(1)} reshape(bf16[12,2,32,32,32]{3,2,4,1,0:T(8,128)(2,1)} %copy.45) | data formatting | bytes 3145728 | tf_op jit(solution)/shard_map/reshape | solution.py:95
  332.1 17.3 %fusion.22 = f32[12,2,32,1024]{3,2,1,0:T(8,128)S(1)} fusion(bf16[12,2,1024,32]{2,3,1,0:T(8,128)(2,1)S(1)} %reshape.94), kind=kOutput, calls=%fused_computation.94 | convolution fusion | flops 1627389952 | bytes 4718592 | tf_op jit(solution)/shard_map/savr,vc->sarc/dot_general | solution.py:102
  349.4 17.2 %fusion.30 = f32[12,2,32,1024]{3,2,1,0:T(8,128)S(1)} fusion(bf16[12,2,1024,32]{2,3,1,0:T(8,128)(2,1)S(1)} %reshape.94), kind=kOutput, calls=%fused_computation.98 | convolution fusion | flops 1626341376 | bytes 4718592 | tf_op jit(solution)/shard_map/savr,vc->sarc/dot_general | solution.py:101
  366.6 1.1 fusion.128
  368.2 11.1 %fusion.19 = bf16[12,32,1024]{2,0,1:T(8,128)(2,1)S(1)} fusion(f32[12,1,32,1024]{3,2,1,0:T(8,128)S(1)} %get-tuple-element.24, f32[12,1,32,1024]{3,2,1,0:T(8,128)S(1)} %get-tuple-element.19, f32[12,1,32,1024]{3,2,1,0:T(8,128)S(1)} %get-tuple-element.25, f32[12,1,32,1024]{3,2,1,0:T(8,128)S(1)} %get-tuple-element.18, f32[12,32,1024]{2,0,1:T(8,128)S(1)} %copy-done.3, ...), kind=kLoop, calls=%fused_computation.90 | loop fusion | flops 3538944 | bytes 8781872 | tf_op jit(solution)/shard_map/convert_element_type | solution.py:107
  380.4 4.5 fusion.130
  385.0 6.8 %fusion.51 = f32[12,64]{1,0:T(8,128)S(1)} fusion(bf16[12,32,1024]{2,0,1:T(8,128)(2,1)S(1)} %fusion.19, bf16[64,32,1024]{2,1,0:T(8,128)(2,1)} %param.6), kind=kOutput, calls=%fused_computation.125 | convolution fusion | flops 50332416 | bytes 4983808 | tf_op jit(solution)/shard_map/dot_general | solution.py:110
  392.0 78.2 %psum.7 = f32[64,64]{1,0:T(8,128)} all-reduce(f32[64,64]{1,0:T(8,128)S(1)} %fusion.90), channel_id=1, replica_groups=mesh['star'=8,'row'=32] {'star','row'}, use_global_device_ids=true, to_apply=%region_4.5 | all-reduce | flops 4096 | bytes 32768 | tf_op jit(solution)/shard_map/psum | solution.py:119
  470.2 2.8 copy.52
  (62 shorter events, 30.6 us)
Async XLA Ops:
  7.2 1.8 copy-start
  16.0 1.3 copy-start.2
  73.9 25.9 %copy-start.4 = (s32[8]{0:T(128)S(1)}, s32[8]{0:T(128)}, u32[]{:S(2)}) copy-start(s32[8]{0:T(128)} %param.8) | copy-start | bytes 100
  87.8 49.9 %all-to-all-start = ((bf16[32,2,12288]{2,1,0:T(2,128)(2,1)}), bf16[32,2,12288]{2,1,0:T(2,128)(2,1)S(1)}, u32[]{:S(2)}, u32[]{:S(2)}) async-start(bf16[32,2,12288]{2,1,0:T(2,128)(2,1)} %reshape.101), calls=%async_computation | async-start | bytes 3145728 | tf_op jit(solution)/shard_map/all_to_all | solution.py:75
  99.8 370.4 %reduce-scatter.2.cloned.1.call-start = ((), (), s32[]{:S(2)}) async-start(), calls=%async_computation.3 | async-start | bytes 9437184 | tf_op jit(solution)/shard_map/reduce_scatter | solution.py:121
  366.6 1.6 copy-start.3
  385.0 88.1 %copy-start.1 = (bf16[64,64]{1,0:T(8,128)(2,1)S(1)}, bf16[64,64]{1,0:T(8,128)(2,1)}, u32[]{:S(2)}) copy-start(bf16[64,64]{1,0:T(8,128)(2,1)} %param.7) | copy-start | bytes 24580
Sparse Core Ops, SparseCore 0:
  385.1 54.6 reduce-scatter.1
